TPU v7x, 256 devices: a whole 4x4x8 slice. The times are simulated.
256 devices in a mesh: occa: 8 (over x, core), occb: 4 (over z_lo), rows: 8 (over z_hi, y).
Axes of the slice: x: 4, y: 4, z: 8 (z_hi: 2, z_lo: 4; z = z_hi * 4 + z_lo), core: 2. Of those that a mesh axis runs over, the one named last changes fastest.
Arguments:
- density: float32 [512, 8, 4, 2, 512], P('rows', 'occa', 'occb'), may hold values from -6 to 6
- operators: float32 [5, 512, 512], P(None, 'rows'), as said below
- rates: float32 [2], replicated, may hold values from 0.05 to 0.5
- coupling: float32 [2, 2], replicated, may hold values from 0.3 to 1
- keep_mask: int32 [8, 4], P('occa', 'occb'), may hold values 0 or 1
Outputs:
- advanced: float32 [512, 8, 4, 2, 512], P('rows', 'occa', 'occb')
Inputs may be any that keep to these rules, and one draw needn't show every extreme that they name: `keep_mask`: 1 keeps an auxiliary matrix in the hierarchy, 0 removes it. `operators`: each of the five matrices is symmetric.
All inputs are finite; a program needn't handle non-finite values. No bound on the sum of `keep_mask` on one device may be relied on, other than what follows from the above.
Results may differ from a plain program's by a relative error of at most 0.00005.
Values sent between devices are 32-bit elements; how exact they have to be, the bound alone decides.
A program may use at most 64 MiB of HBM per device.

v0:
```python
import jax
import jax.numpy as jnp
from jax import lax
from jax.sharding import PartitionSpec as P

TIME_STEP = 0.05
PRECISE = lax.Precision.HIGHEST


def padded(cells, sides, width):
    for axis, dim in sides:
        count = lax.axis_size(axis)
        ends = count - 1
        head = lax.slice_in_dim(cells, 0, width, axis=dim)
        tail = lax.slice_in_dim(cells, cells.shape[dim] - width, cells.shape[dim], axis=dim)
        cells = jnp.concatenate(
            [
                lax.ppermute(tail, axis, [(i, (i + 1) % count) for i in range(ends)]),
                cells,
                lax.ppermute(head, axis, [((i + 1) % count, i) for i in range(ends)]),
            ],
            axis=dim,
        )
    return cells


def neighbours(extended, count_a, count_b):
    return jnp.stack(
        [
            extended[:, 1 : count_a + 1, 1 : count_b + 1],
            extended[:, 2 : count_a + 2, 1 : count_b + 1],
            extended[:, 0:count_a, 1 : count_b + 1],
            extended[:, 1 : count_a + 1, 2 : count_b + 2],
            extended[:, 1 : count_a + 1, 0:count_b],
        ],
        axis=3,
    )


def ladder_factors(occ_a, occ_b, coupling):
    zeros = jnp.zeros_like(occ_a + occ_b)
    up_a = jnp.sqrt(occ_a + 1.0)
    up_b = jnp.sqrt(occ_b + 1.0)
    down_a = jnp.sqrt(occ_a)
    down_b = jnp.sqrt(occ_b)
    factor_re = jnp.stack(
        [zeros, zeros, down_a * coupling[0, 1], zeros, down_b * coupling[1, 1]], axis=-1
    )
    factor_im = jnp.stack(
        [zeros - 1.0, -up_a, -down_a * coupling[0, 0], -up_b, -down_b * coupling[1, 0]], axis=-1
    )
    return (factor_re, factor_im)


def weighted(stacked, factor_re, factor_im):
    part_re = stacked[..., 0, :]
    part_im = stacked[..., 1, :]
    scale_re = factor_re[None, :, :, :, None]
    scale_im = factor_im[None, :, :, :, None]
    return jnp.stack(
        [scale_re * part_re - scale_im * part_im, scale_re * part_im + scale_im * part_re], axis=4
    )


def shards(density, operators, rates, coupling, keep_mask):
    row_count = density.shape[0]
    count_a = density.shape[1]
    count_b = density.shape[2]
    full_ops = lax.all_gather(operators, "rows", axis=1, tiled=True)
    occ_a = (lax.axis_index("occa") * count_a + jnp.arange(count_a)).astype(jnp.float32)[:, None]
    occ_b = (lax.axis_index("occb") * count_b + jnp.arange(count_b)).astype(jnp.float32)[None, :]
    row_start = lax.axis_index("rows") * row_count
    factor_re, factor_im = ladder_factors(occ_a, occ_b, coupling)
    damping = (occ_a * rates[0] + occ_b * rates[1])[None, :, :, None, None]
    kept = keep_mask.astype(jnp.float32)[None, :, :, None, None]

    def derivative(field):
        extended = padded(field, (("occa", 1), ("occb", 2)), 1)
        stacked = neighbours(extended, count_a, count_b)
        right_ops = weighted(stacked, factor_re, -factor_im)
        right_part = jnp.einsum("iabkpc,kcm->iabpm", right_ops, full_ops, precision=PRECISE)
        left_ops = weighted(stacked, factor_re, factor_im)
        op_slice = lax.dynamic_slice_in_dim(full_ops, row_start, row_count, 2)
        left_part = lax.psum_scatter(
            jnp.einsum("kic,cabkpm->iabpm", op_slice, left_ops, precision=PRECISE),
            "rows",
            scatter_dimension=0,
            tiled=True,
        )
        return (left_part + right_part - damping * field) * kept

    start = density * kept
    first = derivative(start)
    second = derivative(first)
    return start + TIME_STEP * first + 0.5 * TIME_STEP * TIME_STEP * second


def solution(mesh):
    placed = (
        P("rows", "occa", "occb", None, None),
        P(None, "rows", None),
        P(),
        P(),
        P("occa", "occb"),
    )
    return jax.shard_map(
        shards,
        mesh=mesh,
        in_specs=placed,
        out_specs=P("rows", "occa", "occb", None, None),
        check_vma=False,
    )
```

profile of v0, /device:TPU:1, one launch (start us, length us, event | category | flops | bytes accessed | tf_op | source)
XLA Modules:
  0.0 391.2 jit_solution(12021623194083770563)
XLA Ops:
  6.5 0.7 all-gather.2.cloned.1.call-update
  8.0 1.0 bitcast_dynamic-update-slice_fusion.5
  9.0 4.5 %collective-permute-start.1 = (f32[64,1,1,2,512]{4,0,3,2,1:T(8,128)S(1)}, f32[64,1,1,2,512]{4,0,3,2,1:T(8,128)S(1)}, u32[]{:S(2)}, u32[]{:S(2)}) collective-permute-start(f32[64,1,1,2,512]{4,0,3,2,1:T(8,128)S(1)} %get-tuple-element.6), channel_id=1, source_target_pairs={{0,32},{32,64},{64,96},{96,128},{128,160},{160,192},{192,224},{1,3... | collective-permute-start | bytes 786440 | tf_op jit(solution)/shard_map/ppermute | solution.py:18
  13.5 1.9 collective-permute-start
  15.4 1.3 collective-permute-done.1
  16.8 4.4 %collective-permute-done = f32[64,1,1,2,512]{4,0,3,2,1:T(8,128)S(1)} collective-permute-done((f32[64,1,1,2,512]{4,0,3,2,1:T(8,128)S(1)}, f32[64,1,1,2,512]{4,0,3,2,1:T(8,128)S(1)}, u32[]{:S(2)}, u32[]{:S(2)}) %collective-permute-start) | collective-permute-done | bytes 262176 | tf_op jit(solution)/shard_map/ppermute | solution.py:20
  21.3 1.3 collective-permute-start.2
  22.7 0.7 fusion.59
  26.1 4.2 %collective-permute-start.3 = (f32[64,3,1,2,512]{4,0,3,2,1:T(8,128)S(1)}, f32[64,3,1,2,512]{4,0,3,2,1:T(8,128)S(1)}, u32[]{:S(2)}, u32[]{:S(2)}) collective-permute-start(f32[64,3,1,2,512]{4,0,3,2,1:T(8,128)S(1)} %pad_maximum_fusion), channel_id=1, source_target_pairs={{0,8},{8,16},{16,24},{1,9},{9,17},{17,25},{2,10},{10,18},{18,26},{... | collective-permute-start | bytes 2359304 | tf_op jit(solution)/shard_map/ppermute | solution.py:18
  30.5 22.6 %collective-permute-done.2 = f32[64,3,1,2,512]{4,0,3,2,1:T(8,128)} collective-permute-done((f32[64,3,1,2,512]{4,0,3,2,1:T(8,128)S(1)}, f32[64,3,1,2,512]{4,0,3,2,1:T(8,128)}, u32[]{:S(2)}, u32[]{:S(2)}) %collective-permute-start.2) | collective-permute-done | bytes 786464 | tf_op jit(solution)/shard_map/ppermute | solution.py:20
  53.1 1.0 fusion.49
  54.1 4.0 %collective-permute-done.3 = f32[64,3,1,2,512]{4,0,3,2,1:T(8,128)S(1)} collective-permute-done((f32[64,3,1,2,512]{4,0,3,2,1:T(8,128)S(1)}, f32[64,3,1,2,512]{4,0,3,2,1:T(8,128)S(1)}, u32[]{:S(2)}, u32[]{:S(2)}) %collective-permute-start.3) | collective-permute-done | bytes 786464 | tf_op jit(solution)/shard_map/ppermute | solution.py:18
  58.1 1.1 copy-done
  59.2 1.8 multiply_subtract_fusion.2
  60.9 82.7 %all-gather.2.cloned.1.call-done = f32[5,512,512]{2,1,0:T(8,128)} async-done(((f32[5,64,512]{2,1,0:T(8,128)}), f32[5,512,512]{2,1,0:T(8,128)}) %all-gather.2.cloned.1.call-update) | async-done | bytes 5242896 | tf_op jit(solution)/shard_map/all_gather | solution.py:69
  143.6 6.4 %convolution_bitcast_fusion.1 = f32[512,1,1,2,512]{4,0,3,2,1:T(8,128)} fusion(f32[64,1,1,5,1,512]{5,0,3,4,2,1:T(8,128)S(1)} %get-tuple-element.17, f32[64,1,1,5,1,512]{5,0,3,4,2,1:T(8,128)S(1)} %get-tuple-element.18, f32[5,512,512]{2,1,0:T(8,128)} %all-gather.2.cloned.1.call-done, s32[]{:T(128)S(6)} %select_n.4), kind=kOutput, calls=%fused_computation.5 | convolution fusion | flops 2013593600 | bytes 4718596 | tf_op jit(solution)/shard_map/kic,cabkpm->iabpm/dot_general | solution.py:85
  150.1 0.6 copy-done.2
  150.7 0.6 fusion.60
  152.5 87.0 %reduce-scatter.3.cloned.1.call-done = f32[64,1,1,2,512]{4,0,3,2,1:T(8,128)} async-done(((f32[512,1,1,2,512]{4,0,3,2,1:T(8,128)}), f32[64,1,1,2,512]{4,0,3,2,1:T(8,128)}) %reduce-scatter.3.cloned.1.call-update) | async-done | bytes 262160 | tf_op jit(solution)/shard_map/reduce_scatter | solution.py:84
  239.5 5.5 %bitcast_dynamic-update-slice_fusion.2 = (f32[64,1,1,5,2,512]{5,0,3,4,2,1:T(8,128)S(1)}, f32[64,1,1,2,512]{4,0,3,2,1:T(8,128)S(1)}) fusion(f32[]{:T(128)} %bitcast, f32[64,1,1,2,512]{4,0,3,2,1:T(8,128)S(1)} %get-tuple-element.6, f32[]{:T(128)} %bitcast.30, f32[64,1,1,2,512]{4,0,3,2,1:T(8,128)} %reduce-scatter.3.cloned.1.call-done, ...), kind=kOutput, calls=%fused_computation.54 | convolution fusion | flops 2013855744 | bytes 7602184 | tf_op jit(solution)/shard_map/iabkpc,kcm->iabpm/dot_general | solution.py:81
  245.1 5.2 %collective-permute-start.5 = (f32[64,1,1,2,512]{4,0,3,2,1:T(8,128)S(1)}, f32[64,1,1,2,512]{4,0,3,2,1:T(8,128)S(1)}, u32[]{:S(2)}, u32[]{:S(2)}) collective-permute-start(f32[64,1,1,2,512]{4,0,3,2,1:T(8,128)S(1)} %get-tuple-element.26), channel_id=1, source_target_pairs={{0,32},{32,64},{64,96},{96,128},{128,160},{160,192},{192,224},{1,3... | collective-permute-start | bytes 786440 | tf_op jit(solution)/shard_map/ppermute | solution.py:18
  250.2 1.9 collective-permute-start.4
  252.2 1.4 collective-permute-done.5
  253.5 4.4 %collective-permute-done.4 = f32[64,1,1,2,512]{4,0,3,2,1:T(8,128)S(1)} collective-permute-done((f32[64,1,1,2,512]{4,0,3,2,1:T(8,128)S(1)}, f32[64,1,1,2,512]{4,0,3,2,1:T(8,128)S(1)}, u32[]{:S(2)}, u32[]{:S(2)}) %collective-permute-start.4) | collective-permute-done | bytes 262176 | tf_op jit(solution)/shard_map/ppermute | solution.py:20
  258.0 1.3 collective-permute-start.6
  259.3 4.2 %collective-permute-start.7 = (f32[64,3,1,2,512]{4,0,3,2,1:T(8,128)S(1)}, f32[64,3,1,2,512]{4,0,3,2,1:T(8,128)S(1)}, u32[]{:S(2)}, u32[]{:S(2)}) collective-permute-start(f32[64,3,1,2,512]{4,0,3,2,1:T(8,128)S(1)} %pad_maximum_fusion.1), channel_id=1, source_target_pairs={{0,8},{8,16},{16,24},{1,9},{9,17},{17,25},{2,10},{10,18},{18,26},{... | collective-permute-start | bytes 2359304 | tf_op jit(solution)/shard_map/ppermute | solution.py:18
  263.6 11.8 %collective-permute-done.6 = f32[64,3,1,2,512]{4,0,3,2,1:T(8,128)S(1)} collective-permute-done((f32[64,3,1,2,512]{4,0,3,2,1:T(8,128)S(1)}, f32[64,3,1,2,512]{4,0,3,2,1:T(8,128)S(1)}, u32[]{:S(2)}, u32[]{:S(2)}) %collective-permute-start.6) | collective-permute-done | bytes 786464 | tf_op jit(solution)/shard_map/ppermute | solution.py:20
  275.4 1.7 collective-permute-done.7
  277.5 6.4 %convolution_bitcast_fusion = f32[512,1,1,2,512]{4,0,3,2,1:T(8,128)} fusion(f32[64,1,1,5,1,512]{5,0,3,4,2,1:T(8,128)S(1)} %get-tuple-element.15, f32[64,1,1,5,1,512]{5,0,3,4,2,1:T(8,128)S(1)} %get-tuple-element.16, f32[5,512,512]{2,1,0:T(8,128)} %all-gather.2.cloned.1.call-done, s32[]{:T(128)S(6)} %select_n.4), kind=kOutput, calls=%fused_computation.4 | convolution fusion | flops 2013593600 | bytes 4718596 | tf_op jit(solution)/shard_map/kic,cabkpm->iabpm/dot_general | solution.py:85
  283.9 94.3 %reduce-scatter.5.cloned.1.call-done = f32[64,1,1,2,512]{4,0,3,2,1:T(8,128)} async-done(((f32[512,1,1,2,512]{4,0,3,2,1:T(8,128)}), f32[64,1,1,2,512]{4,0,3,2,1:T(8,128)}) %reduce-scatter.5.cloned.1.call-update) | async-done | bytes 262160 | tf_op jit(solution)/shard_map/reduce_scatter | solution.py:84
  378.2 5.5 %fusion.34 = f32[64,1,1,2,512]{4,0,3,2,1:T(8,128)S(1)} fusion(f32[64,1,1,2,512]{4,0,3,2,1:T(8,128)} %reduce-scatter.5.cloned.1.call-done, f32[5,512,512]{2,1,0:T(8,128)} %all-gather.2.cloned.1.call-done, f32[64,1,1,5,1,512]{5,0,3,4,2,1:T(8,128)S(1)} %get-tuple-element.8, f32[64,1,1,5,1,512]{5,0,3,4,2,1:T(8,128)S(1)} %get-tuple-element.7, ...), kind=kOutput, calls=%fused_computation.28 | convolution fusion | flops 2014117888 | bytes 7602184 | tf_op jit(solution)/shard_map/iabkpc,kcm->iabpm/dot_general | solution.py:81
  383.7 0.9 copy.25
  (24 shorter events, 1.0 us)
Async XLA Ops:
  6.5 137.1 %all-gather.2.cloned.1.call-start = ((), (), s32[]{:S(2)}) async-start(), calls=%async_computation.2 | async-start | bytes 5898240 | tf_op jit(solution)/shard_map/all_gather | solution.py:69
  7.3 15.5 %copy-start.1 = (f32[2,2]{1,0:T(2,128)S(1)}, f32[2,2]{1,0:T(2,128)}, u32[]{:S(2)}) copy-start(f32[2,2]{1,0:T(2,128)} %param.8) | copy-start | bytes 52
  7.3 232.3 %reduce-scatter.3.cloned.1.call-start = ((), (), s32[]{:S(2)}) async-start(), calls=%async_computation.3 | async-start | bytes 2359296 | tf_op jit(solution)/shard_map/reduce_scatter | solution.py:84
  9.0 7.8 %collective-permute-start.1 = (f32[64,1,1,2,512]{4,0,3,2,1:T(8,128)S(1)}, f32[64,1,1,2,512]{4,0,3,2,1:T(8,128)S(1)}, u32[]{:S(2)}, u32[]{:S(2)}) collective-permute-start(f32[64,1,1,2,512]{4,0,3,2,1:T(8,128)S(1)} %get-tuple-element.6), channel_id=1, source_target_pairs={{0,32},{32,64},{64,96},{96,128},{128,160},{160,192},{192,224},{1,3... | collective-permute-start | bytes 786440 | tf_op jit(solution)/shard_map/ppermute | solution.py:18
  13.5 7.7 %collective-permute-start = (f32[64,1,1,2,512]{4,0,3,2,1:T(8,128)S(1)}, f32[64,1,1,2,512]{4,0,3,2,1:T(8,128)S(1)}, u32[]{:S(2)}, u32[]{:S(2)}) collective-permute-start(f32[64,1,1,2,512]{4,0,3,2,1:T(8,128)S(1)} %get-tuple-element.6), channel_id=1, source_target_pairs={{32,0},{64,32},{96,64},{128,96},{160,128},{192,160},{224,192},{33,... | collective-permute-start | bytes 786440 | tf_op jit(solution)/shard_map/ppermute | solution.py:20
  21.3 31.8 %collective-permute-start.2 = (f32[64,3,1,2,512]{4,0,3,2,1:T(8,128)S(1)}, f32[64,3,1,2,512]{4,0,3,2,1:T(8,128)}, u32[]{:S(2)}, u32[]{:S(2)}) collective-permute-start(f32[64,3,1,2,512]{4,0,3,2,1:T(8,128)S(1)} %pad_maximum_fusion), channel_id=1, source_target_pairs={{8,0},{16,8},{24,16},{9,1},{17,9},{25,17},{10,2},{18,10},{26,18},{... | collective-permute-start | bytes 2359304 | tf_op jit(solution)/shard_map/ppermute | solution.py:20
  26.1 31.9 %collective-permute-start.3 = (f32[64,3,1,2,512]{4,0,3,2,1:T(8,128)S(1)}, f32[64,3,1,2,512]{4,0,3,2,1:T(8,128)S(1)}, u32[]{:S(2)}, u32[]{:S(2)}) collective-permute-start(f32[64,3,1,2,512]{4,0,3,2,1:T(8,128)S(1)} %pad_maximum_fusion), channel_id=1, source_target_pairs={{0,8},{8,16},{16,24},{1,9},{9,17},{17,25},{2,10},{10,18},{18,26},{... | collective-permute-start | bytes 2359304 | tf_op jit(solution)/shard_map/ppermute | solution.py:18
  58.1 1.1 copy-start
  150.0 0.7 copy-start.2
  150.1 228.1 %reduce-scatter.5.cloned.1.call-start = ((), (), s32[]{:S(2)}) async-start(), calls=%async_computation.4 | async-start | bytes 2359296 | tf_op jit(solution)/shard_map/reduce_scatter | solution.py:84
  245.1 8.5 %collective-permute-start.5 = (f32[64,1,1,2,512]{4,0,3,2,1:T(8,128)S(1)}, f32[64,1,1,2,512]{4,0,3,2,1:T(8,128)S(1)}, u32[]{:S(2)}, u32[]{:S(2)}) collective-permute-start(f32[64,1,1,2,512]{4,0,3,2,1:T(8,128)S(1)} %get-tuple-element.26), channel_id=1, source_target_pairs={{0,32},{32,64},{64,96},{96,128},{128,160},{160,192},{192,224},{1,3... | collective-permute-start | bytes 786440 | tf_op jit(solution)/shard_map/ppermute | solution.py:18
  250.2 7.7 %collective-permute-start.4 = (f32[64,1,1,2,512]{4,0,3,2,1:T(8,128)S(1)}, f32[64,1,1,2,512]{4,0,3,2,1:T(8,128)S(1)}, u32[]{:S(2)}, u32[]{:S(2)}) collective-permute-start(f32[64,1,1,2,512]{4,0,3,2,1:T(8,128)S(1)} %get-tuple-element.26), channel_id=1, source_target_pairs={{32,0},{64,32},{96,64},{128,96},{160,128},{192,160},{224,192},{33,... | collective-permute-start | bytes 786440 | tf_op jit(solution)/shard_map/ppermute | solution.py:20
  258.0 17.4 %collective-permute-start.6 = (f32[64,3,1,2,512]{4,0,3,2,1:T(8,128)S(1)}, f32[64,3,1,2,512]{4,0,3,2,1:T(8,128)S(1)}, u32[]{:S(2)}, u32[]{:S(2)}) collective-permute-start(f32[64,3,1,2,512]{4,0,3,2,1:T(8,128)S(1)} %pad_maximum_fusion.1), channel_id=1, source_target_pairs={{8,0},{16,8},{24,16},{9,1},{17,9},{25,17},{10,2},{18,10},{26,18},{... | collective-permute-start | bytes 2359304 | tf_op jit(solution)/shard_map/ppermute | solution.py:20
  259.3 17.8 %collective-permute-start.7 = (f32[64,3,1,2,512]{4,0,3,2,1:T(8,128)S(1)}, f32[64,3,1,2,512]{4,0,3,2,1:T(8,128)S(1)}, u32[]{:S(2)}, u32[]{:S(2)}) collective-permute-start(f32[64,3,1,2,512]{4,0,3,2,1:T(8,128)S(1)} %pad_maximum_fusion.1), channel_id=1, source_target_pairs={{0,8},{8,16},{16,24},{1,9},{9,17},{17,25},{2,10},{10,18},{18,26},{... | collective-permute-start | bytes 2359304 | tf_op jit(solution)/shard_map/ppermute | solution.py:18
Sparse Core Ops, SparseCore 0:
  10.0 133.6 all-gather.1
  150.2 89.2 reduce-scatter.2
  284.0 94.0 reduce-scatter.4
where the time goes:
time: 392 us; the launch traced here: 391 us
  waiting for transfers between devices  316 us (81%)
  starting transfers between devices  24.6 us (6%)
  matrix products  23.9 us (6%)
  between operations  17.8 us (5%)
  local copies, waits for them, and re-layouts  5.2 us (1%)
    reduce_scatter x2, waiting for transfers between devices, derivative(): lax.psum_scatter(jnp.einsum('kic,cabkpm->iabpm', op_slice, left_ops, prec...  181 us
    all_gather x1, waiting for transfers between devices, shards(): full_ops = lax.all_gather(operators, 'rows', axis=1, tiled=True)  82.7 us
    ppermute x4, waiting for transfers between devices, padded(): lax.ppermute(head, axis, [((i + 1) % count, i) for i in range(ends)])  43.2 us
    ppermute x4, starting transfers between devices, padded(): lax.ppermute(tail, axis, [(i, (i + 1) % count) for i in range(ends)])  18.1 us
    dot_general x2, matrix products, derivative(): jnp.einsum('kic,cabkpm->iabpm', op_slice, left_ops, precision=PRECISE)  12.8 us
    dot_general x2, matrix products, derivative(): jnp.einsum('iabkpc,kcm->iabpm', right_ops, full_ops, precision=PRECISE)  11.1 us
    ppermute x4, waiting for transfers between devices, padded(): lax.ppermute(tail, axis, [(i, (i + 1) % count) for i in range(ends)])  8.41 us
  transfers between devices with their start and end apart: 11, of which 11 were waited for; matrix products, arithmetic and copies ran while one was open for 1% of the time, Pallas kernels for 0%

commit v1 on v0

v1 whole, which is shorter than its diff:
```python
import jax
import jax.numpy as jnp
from jax import lax
from jax.experimental import pallas as pl
from jax.experimental.pallas import tpu as pltpu
from jax.sharding import PartitionSpec as P

TIME_STEP = 0.05
MESH = pl.DeviceIdType.MESH
F32 = jnp.float32
BF16 = jnp.bfloat16
SITES = 512
OPS = 5
ROWS = 64
COLS = 16
PLANE = 32
COUNT_A = 8
COUNT_B = 4
OWN = COUNT_B


def split(value):
    high = value.astype(BF16)
    low = (value - high.astype(F32)).astype(BF16)
    return high, low


def kernel(
    par, dens, ops, keep, out,
    own, oth, whi, wlo, ghl,
    sent_r, cols_buf, held_c, pack, first_r, first_c,
    near_r, near_c, keeps,
    a_send, a_recv, n_send, n_recv, k_send, k_recv, o_send, o_recv,
):
    ia = lax.axis_index("occa")
    ib = lax.axis_index("occb")
    ir = lax.axis_index("rows")
    half = ir // 4
    iy = lax.rem(ir, 4)
    ix = ia // 2
    core = lax.rem(ia, 2)
    iz = half * 4 + ib
    me_col = iz * 4 + iy
    me_row = ib * 8 + ir

    def a_dev(step):
        return {"occa": lax.rem(ia + step + COUNT_A, COUNT_A)}

    def z_dev(step):
        z = lax.rem(iz + step + 8, 8)
        return {"occb": lax.rem(z, 4), "rows": (z // 4) * 4 + iy}

    def y_dev(step):
        return {"rows": half * 4 + lax.rem(iy + step, 4)}

    def partner(j):
        z = lax.rem(iz + j // 4, 8)
        y = lax.rem(iy + lax.rem(j, 4), 4)
        b = lax.rem(z, 4)
        r = (z // 4) * 4 + y
        return {"occb": b, "rows": r}, z * 4 + y, b * 8 + r

    sibling = {"occa": ix * 2 + 1 - core}

    def remote(src, dst, send, recv, dev):
        return pltpu.make_async_remote_copy(
            src_ref=src, dst_ref=dst, send_sem=send, recv_sem=recv, device_id=dev, device_id_type=MESH
        )

    def block(index):
        return pl.ds(pl.multiple_of(index * COLS, COLS), COLS)

    def to_columns(slot, j):
        dev, col, row = partner(j)
        return remote(sent_r.at[slot, block(col)], cols_buf.at[slot, block(me_row)],
                      a_send.at[slot, j], a_recv.at[slot, me_row], dev)

    def to_rows(slot, j):
        dev, col, row = partner(j)
        return remote(pack.at[slot - 2, block(row)], cols_buf.at[slot, block(me_col)],
                      a_send.at[slot, j], a_recv.at[slot, me_col], dev)

    def start_columns(slot):
        def body(j, carry):
            to_columns(slot, j).start()
            return carry
        lax.fori_loop(1, PLANE, body, 0)
        cols_buf[slot, block(me_row), :] = sent_r[slot, block(me_col), :]

    def start_rows(slot):
        def body(j, carry):
            to_rows(slot, j).start()
            return carry
        lax.fori_loop(1, PLANE, body, 0)
        cols_buf[slot, block(me_col), :] = pack[slot - 2, block(me_row), :]

    def finish_recv(slot, by_row):
        def body(j, carry):
            dev, col, row = partner(j)
            index = row if by_row else col
            piece = cols_buf.at[slot, block(index)]
            remote(piece, piece, a_send.at[slot, j], a_recv.at[slot, index], dev).wait_recv()
            return carry
        lax.fori_loop(1, PLANE, body, 0)

    def finish_send(slot):
        def body(j, carry):
            (to_columns if slot < 2 else to_rows)(slot, j).wait_send()
            return carry
        lax.fori_loop(1, PLANE, body, 0)

    lanes = lax.broadcasted_iota(jnp.int32, (COLS, 128), 1) < 64

    def unpack(slot):
        parts = []
        for b in range(COUNT_B):
            real, imag = [], []
            for t in range(4):
                q = (b * 8 + 2 * t) * COLS
                even = cols_buf[slot, q:q + COLS, :]
                odd = cols_buf[slot, q + COLS:q + 2 * COLS, :]
                real.append(jnp.where(lanes, even, pltpu.roll(odd, 64, 1)))
                imag.append(jnp.where(lanes, pltpu.roll(even, 64, 1), odd))
            parts.append(jnp.concatenate(real, axis=1))
            parts.append(jnp.concatenate(imag, axis=1))
        return jnp.concatenate(parts, axis=0)

    def repack(slot, value):
        for b in range(COUNT_B):
            for t in range(4):
                real = value[32 * b:32 * b + COLS, 128 * t:128 * t + 128]
                imag = value[32 * b + COLS:32 * b + 32, 128 * t:128 * t + 128]
                q = (b * 8 + 2 * t) * COLS
                pack[slot - 2, q:q + COLS, :] = jnp.where(lanes, real, pltpu.roll(imag, 64, 1))
                pack[slot - 2, q + COLS:q + 2 * COLS, :] = jnp.where(lanes, pltpu.roll(real, 64, 1), imag)

    def put(k, row, value):
        high, low = split(value)
        count = value.shape[0]
        ghl[row:row + count, k * SITES:(k + 1) * SITES] = high
        ghl[128 + row:128 + row + count, k * SITES:(k + 1) * SITES] = low

    def multiply():
        both = jnp.dot(ghl[...], whi[...], preferred_element_type=F32)
        rest = jnp.dot(ghl[0:128, :], wlo[...], preferred_element_type=F32)
        return both[0:128] + both[128:256] + rest

    def right(center, base):
        fields = [center, near_r.at[base], near_r.at[base + 1], near_r.at[base + 2], near_r.at[base + 3]]
        for k, field in enumerate(fields):
            re, im = field[0:ROWS, :], field[ROWS:128, :]
            f_re, f_im = par[OWN, 2 * k], par[OWN, 2 * k + 1]
            put(k, 0, f_re * re + f_im * im)
            put(k, ROWS, f_re * im - f_im * re)
        return multiply()

    def left(center, base):
        for b in range(COUNT_B):
            for k in range(OPS):
                source, at = center, b
                if k == 1:
                    source = near_c.at[base]
                elif k == 2:
                    source = near_c.at[base + 1]
                elif k == 3:
                    at = min(b + 1, COUNT_B - 1)
                elif k == 4:
                    at = max(b - 1, 0)
                re = source[32 * at:32 * at + COLS, :]
                im = source[32 * at + COLS:32 * at + 32, :]
                f_re, f_im = par[b, 2 * k], par[b, 2 * k + 1]
                put(k, 32 * b, f_re * re - f_im * im)
                put(k, 32 * b + COLS, f_re * im + f_im * re)
        return multiply()

    def near_copy(kind, index, src, dst, dev):
        return remote(src, dst, n_send.at[kind, index], n_recv.at[kind, index], dev)

    def row_moves(kind, src):
        base = 4 * kind
        return [
            near_copy(kind, 0, src, near_r.at[base], a_dev(-1)),
            near_copy(kind, 1, src, near_r.at[base + 1], a_dev(1)),
            near_copy(kind, 2, src, near_r.at[base + 2], z_dev(-1)),
            near_copy(kind, 3, src, near_r.at[base + 3], z_dev(1)),
        ]

    def col_moves(kind, src):
        base = 2 * kind
        return [
            near_copy(2 + kind, 0, src, near_c.at[base], a_dev(-1)),
            near_copy(2 + kind, 1, src, near_c.at[base + 1], a_dev(1)),
        ]

    def eight(index):
        return pl.ds(pl.multiple_of(index * 8, 8), 8)

    def thirty_two(index):
        return pl.ds(pl.multiple_of(index * 32, 32), 32)

    def wide(index):
        return pl.ds(pl.multiple_of(index * 256, 256), 256)

    share = core * 4 + ix
    half_z = remote(ops.at[:, eight(share), wide(half)], oth.at[iy, :, eight(share), :],
                    o_send.at[0], o_recv.at[0], z_dev(4))
    half_y = [remote(oth.at[iy, :, eight(share), :], oth.at[iy, :, eight(share), :],
                     o_send.at[s], o_recv.at[s], y_dev(s)) for s in (1, 2, 3)]
    half_x = [remote(oth.at[:, :, eight(share), :], oth.at[:, :, eight(share), :],
                     o_send.at[3 + s], o_recv.at[3 + s], a_dev(2 * s)) for s in (1, 2, 3)]
    half_c = remote(oth.at[:, :, thirty_two(core), :], oth.at[:, :, thirty_two(core), :],
                    o_send.at[7], o_recv.at[7], sibling)
    own_y = [remote(ops.at[:, thirty_two(core), :], own.at[iy, :, thirty_two(core), :],
                    o_send.at[7 + s], o_recv.at[7 + s], y_dev(s)) for s in (1, 2, 3)]

    def own_c(s):
        y = lax.rem(iy + 4 - s, 4)
        return remote(own.at[y, :, thirty_two(core), :], own.at[y, :, thirty_two(core), :],
                      o_send.at[10 + s], o_recv.at[10 + s], sibling)

    keep_moves = [remote(keep, keeps.at[ib], k_send.at[s], k_recv.at[s],
                         {"occb": lax.rem(ib + s, COUNT_B)}) for s in (1, 2, 3)]

    barrier = pltpu.get_barrier_semaphore()

    def greet(j, carry):
        dev, col, row = partner(j)
        pl.semaphore_signal(barrier, inc=1, device_id=dev, device_id_type=MESH)
        return carry

    lax.fori_loop(1, PLANE, greet, 0)
    for step in (1, -1, 2, -2, 4):
        pl.semaphore_signal(barrier, inc=1, device_id=a_dev(step), device_id_type=MESH)
    sent_r[0] = dens[...].T
    pl.semaphore_wait(barrier, PLANE - 1 + 5)

    half_z.start()
    start_columns(0)
    for copy in keep_moves:
        copy.start()
    for copy in own_y:
        copy.start()
    start_moves = row_moves(0, dens)
    for copy in start_moves:
        copy.start()
    keeps[ib] = keep[...]

    def put_operator(y, own_rows, other_rows):
        base = half * 256 + y * ROWS
        for k in range(OPS):
            at = pl.ds(pl.multiple_of(k * SITES + base, ROWS), ROWS)
            high, low = split(own_rows[k])
            whi[at, :] = high
            wlo[at, :] = low

    half_z.wait_recv()
    for copy in half_y:
        copy.start()

    put_operator(iy, ops, None)

    for copy in half_y:
        copy.wait_recv()
    for copy in half_y:
        copy.wait_send()
    half_x_started = half_x
    for copy in half_x_started:
        copy.start()

    finish_recv(0, True)
    held_c[...] = unpack(0)
    start_cols = col_moves(0, held_c)
    for copy in start_cols:
        copy.start()

    own_moves = []
    for s in (1, 2, 3):
        own_y[s - 1].wait_recv()
        copy = own_c(s)
        copy.start()
        own_moves.append(copy)
    for copy in half_x:
        copy.wait_recv()
    for copy in half_x:
        copy.wait_send()
    half_c.start()

    for s in (1, 2, 3):
        y = lax.rem(iy + 4 - s, 4)
        own_moves[s - 1].wait_recv()
        put_operator(y, own.at[y], None)

    for k in range(OPS):
        source = pl.ds(pl.multiple_of(k * SITES + half * 256, 256), 256)
        target = pl.ds(pl.multiple_of(k * SITES + (1 - half) * 256, 256), 256)
        whi[target, wide(half)] = whi[source, wide(1 - half)].T
        wlo[target, wide(half)] = wlo[source, wide(1 - half)].T
    half_c.wait_recv()
    for k in range(OPS):
        for y in range(4):
            at = pl.ds(pl.multiple_of(k * SITES + (1 - half) * 256 + y * ROWS, ROWS), ROWS)
            high, low = split(oth[y, k])
            whi[at, wide(1 - half)] = high
            wlo[at, wide(1 - half)] = low

    for copy in start_moves:
        copy.wait_recv()
    kept = par[OWN, 11]
    damp = par[OWN, 10]
    first_r[...] = kept * (right(dens, 0) - damp * dens[...])
    sent_r[1] = first_r[...].T
    start_columns(1)

    for copy in start_cols:
        copy.wait_recv()
    for copy in keep_moves:
        copy.wait_recv()
    kept_c = jnp.concatenate(
        [jnp.broadcast_to(keeps[b, 0:1, 0:1], (2 * COLS, SITES)) for b in range(COUNT_B)], axis=0
    )
    first_c[...] = kept_c * left(held_c, 0)
    repack(2, first_c[...])
    start_rows(2)

    finish_recv(1, True)
    first_c[...] += unpack(1)
    next_cols = col_moves(1, first_c)
    for copy in next_cols:
        copy.start()
    finish_recv(2, False)
    first_r[...] += cols_buf[2].T
    next_moves = row_moves(1, first_r)
    for copy in next_moves:
        copy.start()

    for copy in next_cols:
        copy.wait_recv()
    repack(3, left(first_c, 2))
    start_rows(3)

    for copy in next_moves:
        copy.wait_recv()
    second = right(first_r, 4) - damp * first_r[...]
    finish_recv(3, False)
    second = kept * (second + cols_buf[3].T)
    out[...] = dens[...] + TIME_STEP * first_r[...] + (0.5 * TIME_STEP * TIME_STEP) * second

    half_z.wait_send()
    for slot in range(4):
        finish_send(slot)
    half_c.wait_send()
    for copy in keep_moves + own_y + own_moves + start_moves + start_cols + next_cols + next_moves:
        copy.wait_send()


def parameters(rates, coupling, keep_mask):
    occ_a = lax.axis_index("occa").astype(F32)
    own_b = lax.axis_index("occb")
    index_b = jnp.concatenate([jnp.arange(COUNT_B), own_b[None]])
    occ_b = index_b.astype(F32)
    ones = jnp.ones_like(occ_b)
    zeros = jnp.zeros_like(occ_b)
    up_a = jnp.where(occ_a < COUNT_A - 1, jnp.sqrt(occ_a + 1.0), 0.0) * ones
    up_b = jnp.where(occ_b < COUNT_B - 1, jnp.sqrt(occ_b + 1.0), 0.0)
    down_a = jnp.sqrt(occ_a) * ones
    down_b = jnp.sqrt(occ_b)
    damping = occ_a * rates[0] + occ_b * rates[1]
    kept = keep_mask[0, 0].astype(F32) * ones
    return jnp.stack(
        [
            zeros, -ones,
            zeros, -up_a,
            down_a * coupling[0, 1], -down_a * coupling[0, 0],
            zeros, -up_b,
            down_b * coupling[1, 1], -down_b * coupling[1, 0],
            damping, kept,
        ],
        axis=1,
    )


def shards(density, operators, rates, coupling, keep_mask):
    kept = keep_mask[0, 0].astype(F32)
    start = (density[:, 0, 0] * kept).transpose(1, 0, 2).reshape(2 * ROWS, SITES)
    keep = jnp.full((8, 128), kept, F32)
    par = parameters(rates, coupling, keep_mask)
    vmem = pl.BlockSpec(memory_space=pltpu.VMEM)
    dma = pltpu.SemaphoreType.DMA
    result = pl.pallas_call(
        kernel,
        out_shape=jax.ShapeDtypeStruct((2 * ROWS, SITES), F32),
        in_specs=[pl.BlockSpec(memory_space=pltpu.SMEM), vmem, vmem, vmem],
        out_specs=vmem,
        scratch_shapes=[
            pltpu.VMEM((4, OPS, ROWS, SITES), F32),
            pltpu.VMEM((4, OPS, ROWS, SITES // 2), F32),
            pltpu.VMEM((OPS * SITES, SITES), BF16),
            pltpu.VMEM((OPS * SITES, SITES), BF16),
            pltpu.VMEM((256, OPS * SITES), BF16),
            pltpu.VMEM((2, SITES, 128), F32),
            pltpu.VMEM((4, SITES, 128), F32),
            pltpu.VMEM((128, SITES), F32),
            pltpu.VMEM((2, SITES, 128), F32),
            pltpu.VMEM((128, SITES), F32),
            pltpu.VMEM((128, SITES), F32),
            pltpu.VMEM((8, 128, SITES), F32),
            pltpu.VMEM((4, 128, SITES), F32),
            pltpu.VMEM((COUNT_B, 8, 128), F32),
            dma((4, PLANE)),
            dma((4, PLANE)),
            dma((4, 4)),
            dma((4, 4)),
            dma((4,)),
            dma((4,)),
            dma((14,)),
            dma((14,)),
        ],
        compiler_params=pltpu.CompilerParams(
            collective_id=0, has_side_effects=True, vmem_limit_bytes=48 << 20
        ),
    )(par, start, operators, keep)
    return result.reshape(2, ROWS, SITES).transpose(1, 0, 2).reshape(density.shape)


def solution(mesh):
    placed = (
        P("rows", "occa", "occb", None, None),
        P(None, "rows", None),
        P(),
        P(),
        P("occa", "occb"),
    )
    return jax.shard_map(
        shards,
        mesh=mesh,
        in_specs=placed,
        out_specs=P("rows", "occa", "occb", None, None),
        check_vma=False,
    )
```

time: 392 us -> 92.5 us (0.24)
  waiting for transfers between devices: 316 us -> 0 us
  Pallas kernels: 0 us -> 82.7 us
  starting transfers between devices: 24.6 us -> 0 us
  matrix products: 23.9 us -> 0 us
  between operations: 17.8 us -> 2.78 us
    reduce_scatter x2 -> x0, waiting for transfers between devices: 181 us -> none  [derivative(): lax.psum_scatter(jnp.einsum('kic,cabkpm->iabpm', op_slice, left_ops, prec...]
    all_gather x1 -> x0, waiting for transfers between devices: 82.7 us -> none  [shards(): full_ops = lax.all_gather(operators, 'rows', axis=1, tiled=True)]
    pallas_call x0 -> x1, Pallas kernels: none -> 82.7 us  [shards(): pl.pallas_call(kernel, out_shape=jax.ShapeDtypeStruct((2 * ROWS, SITES),...]
    ppermute x8 -> x0, waiting for transfers between devices: 51.6 us -> none  [the longest x4 43.2 us: padded(): lax.ppermute(head, axis, [((i + 1) % count, i) for i in range(ends)])]
    ppermute x8 -> x0, starting transfers between devices: 24.5 us -> none  [the longest x4 18.1 us: padded(): lax.ppermute(tail, axis, [(i, (i + 1) % count) for i in range(ends)])]
    dot_general x4 -> x0, matrix products: 23.9 us -> none  [the longest x2 12.8 us: derivative(): jnp.einsum('kic,cabkpm->iabpm', op_slice, left_ops, precision=PRECISE)]
  transfers between devices with their start and end apart: 11 -> 0, of which waited for: 11 -> 0; matrix products, arithmetic and copies ran while one was open for 1% -> 0% of each run, Pallas kernels for 0% -> 0%
where the time goes in v1:
time: 92.5 us; the launch traced here: 92.3 us
  Pallas kernels  82.7 us (89%)
  local copies, waits for them, and re-layouts  3.91 us (4%)
  other arithmetic  2.96 us (3%)
  between operations  2.78 us (3%)
    pallas_call x1, Pallas kernels, shards(): pl.pallas_call(kernel, out_shape=jax.ShapeDtypeStruct((2 * ROWS, SITES),...  82.7 us

profile of v1, /device:TPU:1, one launch (start us, length us, event | category | flops | bytes accessed | tf_op | source)
XLA Modules:
  0.0 92.3 jit_solution(3584382510559525734)
XLA Ops:
  0.0 0.0 copy-start
  0.8 0.1 pad_add_fusion
  0.9 1.3 %fusion.2 = (f32[1]{0:T(128)}, f32[1]{0:T(128)}) fusion(f32[2]{0:T(128)} %param.7), kind=kLoop, calls=%fused_computation.10 | loop fusion | bytes 16 | tf_op jit(solution)/shard_map/slice | solution.py:367
  2.9 1.4 %fusion.1 = (f32[1,1]{1,0:T(1,128)}, f32[1,1]{1,0:T(1,128)}, f32[1,1]{1,0:T(1,128)}, f32[1,1]{1,0:T(1,128)}) fusion(f32[2,2]{1,0:T(2,128)} %param.8), kind=kLoop, calls=%fused_computation.9 | loop fusion | bytes 32 | tf_op jit(solution)/shard_map/slice | solution.py:375
  5.6 0.1 copy.8
  5.7 1.8 %multiply_add_fusion = (f32[5,1]{1,0:T(8,128)S(1)}, f32[5,1]{1,0:T(8,128)S(1)}, f32[5,1]{1,0:T(8,128)S(1)}, f32[5,1]{1,0:T(8,128)S(1)}) fusion(s32[5,1]{1,0:T(8,128)S(1)} %copy.8, f32[]{:T(128)} %bitcast.6, f32[]{:T(128)S(6)} %mul.70, f32[]{:T(128)} %bitcast.4, f32[]{:T(128)} %bitcast.3), kind=kLoop, calls=%fused_computation.2 | loop fusion | flops 50 | bytes 116 | tf_op jit(solution)/shard_map/add | solution.py:367
  7.5 0.1 stack.23.par
  7.6 1.0 %multiply_bitcast_fusion = f32[2,64,512]{2,0,1:T(2,128)S(1)} fusion(f32[64,1,1,2,512]{4,3,2,1,0:T(2,128)} %param.5, f32[]{:T(128)} %bitcast.7), kind=kLoop, calls=%fused_computation.1 | loop fusion | flops 65536 | bytes 524292 | tf_op jit(solution)/shard_map/transpose | solution.py:384
  8.7 0.1 copy.9
  8.7 0.0 copy-done
  8.7 82.7 %shard_map.55 = f32[128,512]{1,0:T(8,128)S(1)} custom-call(f32[5,12]{1,0:T(8,128)S(1)} %stack.23.par, f32[128,512]{1,0:T(8,128)S(1)} %bitcast.19, f32[5,64,512]{2,1,0:T(8,128)S(1)} %copy-done, f32[8,128]{1,0:T(8,128)S(1)} %broadcast_in_dim.6.keep), custom_call_target="tpu_custom_call" | custom-call | tf_op jit(solution)/shard_map/pallas_call | solution.py:389
  91.4 0.9 copy.12
  (8 shorter events, 0.0 us)
Async XLA Ops:
  0.0 8.7 %copy-start = (f32[5,64,512]{2,1,0:T(8,128)S(1)}, f32[5,64,512]{2,1,0:T(8,128)}, u32[]{:S(2)}) copy-start(f32[5,64,512]{2,1,0:T(8,128)} %ops.1) | copy-start | bytes 1966084

commit v2 on v1

--- a/solution.py
+++ b/solution.py
@@ -1,3 +1,4 @@
+import math
 import jax
 import jax.numpy as jnp
 from jax import lax
@@ -16,7 +17,6 @@
 PLANE = 32
 COUNT_A = 8
 COUNT_B = 4
-OWN = COUNT_B
 
 
 def split(value):
@@ -25,9 +25,16 @@
     return high, low
 
 
+def root(count):
+    value = jnp.float32(0.0)
+    for n in range(1, COUNT_A):
+        value = jnp.where(count == n, math.sqrt(n), value)
+    return value
+
+
 def kernel(
-    par, dens, ops, keep, out,
-    own, oth, whi, wlo, ghl,
+    rates, coupling, mask, density, ops, out,
+    dens, own, oth, whi, wlo, ghl,
     sent_r, cols_buf, held_c, pack, first_r, first_c,
     near_r, near_c, keeps,
     a_send, a_recv, n_send, n_recv, k_send, k_recv, o_send, o_recv,
@@ -60,6 +67,36 @@
         r = (z // 4) * 4 + y
         return {"occb": b, "rows": r}, z * 4 + y, b * 8 + r
 
+    barrier = pltpu.get_barrier_semaphore()
+
+    def greet(j, carry):
+        pl.semaphore_signal(barrier, inc=1, device_id=partner(j)[0], device_id_type=MESH)
+        return carry
+
+    lax.fori_loop(1, PLANE, greet, 0)
+    for step in (1, -1, 2, -2, 4):
+        pl.semaphore_signal(barrier, inc=1, device_id=a_dev(step), device_id_type=MESH)
+
+    kept = mask[0, 0].astype(F32)
+    for part in range(2):
+        dens[part * ROWS:(part + 1) * ROWS, :] = kept * density[:, part, :]
+    sent_r[0] = dens[...].T
+    keeps[ib] = jnp.full((8, 128), kept, F32)
+    down_a = root(ia)
+    up_a = jnp.where(ia < COUNT_A - 1, root(ia + 1), 0.0)
+    damp = ia.astype(F32) * rates[0] + ib.astype(F32) * rates[1]
+
+    def factors(b):
+        down_b = root(b)
+        up_b = jnp.where(b < COUNT_B - 1, root(b + 1), 0.0)
+        return [
+            (0.0, -1.0),
+            (0.0, -up_a),
+            (down_a * coupling[0, 1], -down_a * coupling[0, 0]),
+            (0.0, -up_b),
+            (down_b * coupling[1, 1], -down_b * coupling[1, 0]),
+        ]
+
     sibling = {"occa": ix * 2 + 1 - core}
 
     def remote(src, dst, send, recv, dev):
@@ -147,15 +184,17 @@
 
     def right(center, base):
         fields = [center, near_r.at[base], near_r.at[base + 1], near_r.at[base + 2], near_r.at[base + 3]]
+        own_factors = factors(ib)
         for k, field in enumerate(fields):
             re, im = field[0:ROWS, :], field[ROWS:128, :]
-            f_re, f_im = par[OWN, 2 * k], par[OWN, 2 * k + 1]
+            f_re, f_im = own_factors[k]
             put(k, 0, f_re * re + f_im * im)
             put(k, ROWS, f_re * im - f_im * re)
         return multiply()
 
     def left(center, base):
         for b in range(COUNT_B):
+            b_factors = factors(b)
             for k in range(OPS):
                 source, at = center, b
                 if k == 1:
@@ -168,7 +207,7 @@
                     at = max(b - 1, 0)
                 re = source[32 * at:32 * at + COLS, :]
                 im = source[32 * at + COLS:32 * at + 32, :]
-                f_re, f_im = par[b, 2 * k], par[b, 2 * k + 1]
+                f_re, f_im = b_factors[k]
                 put(k, 32 * b, f_re * re - f_im * im)
                 put(k, 32 * b + COLS, f_re * im + f_im * re)
         return multiply()
@@ -211,60 +250,53 @@
     half_c = remote(oth.at[:, :, thirty_two(core), :], oth.at[:, :, thirty_two(core), :],
                     o_send.at[7], o_recv.at[7], sibling)
     own_y = [remote(ops.at[:, thirty_two(core), :], own.at[iy, :, thirty_two(core), :],
-                    o_send.at[7 + s], o_recv.at[7 + s], y_dev(s)) for s in (1, 2, 3)]
-
-    def own_c(s):
-        y = lax.rem(iy + 4 - s, 4)
-        return remote(own.at[y, :, thirty_two(core), :], own.at[y, :, thirty_two(core), :],
-                      o_send.at[10 + s], o_recv.at[10 + s], sibling)
-
-    keep_moves = [remote(keep, keeps.at[ib], k_send.at[s], k_recv.at[s],
+                    o_send.at[8 + n], o_recv.at[8 + n], y_dev((1, 3)[n])) for n in range(2)]
+
+    def held(n, rows):
+        return own.at[lax.rem(iy + (3, 1, 2)[n], 4), :, rows, :]
+
+    def sixteen(index):
+        return pl.ds(pl.multiple_of(index * 16, 16), 16)
+
+    passed = [remote(held(n, sixteen(2 * core + n)), held(n, sixteen(2 * core + n)),
+                     o_send.at[10 + n], o_recv.at[10 + n], y_dev((1, 3)[n])) for n in range(2)]
+
+    def own_c(n):
+        return remote(held(n, thirty_two(core)), held(n, thirty_two(core)),
+                      o_send.at[12 + n], o_recv.at[12 + n], sibling)
+
+    keep_moves = [remote(keeps.at[ib], keeps.at[ib], k_send.at[s], k_recv.at[s],
                          {"occb": lax.rem(ib + s, COUNT_B)}) for s in (1, 2, 3)]
 
-    barrier = pltpu.get_barrier_semaphore()
-
-    def greet(j, carry):
-        dev, col, row = partner(j)
-        pl.semaphore_signal(barrier, inc=1, device_id=dev, device_id_type=MESH)
-        return carry
-
-    lax.fori_loop(1, PLANE, greet, 0)
-    for step in (1, -1, 2, -2, 4):
-        pl.semaphore_signal(barrier, inc=1, device_id=a_dev(step), device_id_type=MESH)
-    sent_r[0] = dens[...].T
     pl.semaphore_wait(barrier, PLANE - 1 + 5)
-
     half_z.start()
     start_columns(0)
-    for copy in keep_moves:
-        copy.start()
     for copy in own_y:
         copy.start()
     start_moves = row_moves(0, dens)
-    for copy in start_moves:
-        copy.start()
-    keeps[ib] = keep[...]
-
-    def put_operator(y, own_rows, other_rows):
-        base = half * 256 + y * ROWS
+    for copy in keep_moves + start_moves:
+        copy.start()
+
+    def put_operator(y, rows):
         for k in range(OPS):
-            at = pl.ds(pl.multiple_of(k * SITES + base, ROWS), ROWS)
-            high, low = split(own_rows[k])
+            at = pl.ds(pl.multiple_of(k * SITES + half * 256 + y * ROWS, ROWS), ROWS)
+            high, low = split(rows[k])
             whi[at, :] = high
             wlo[at, :] = low
 
     half_z.wait_recv()
     for copy in half_y:
         copy.start()
-
-    put_operator(iy, ops, None)
-
+    put_operator(iy, ops)
+    own_moves = []
+    for n in range(2):
+        own_y[n].wait_recv()
+        passed[n].start()
+        own_moves.append(own_c(n))
+        own_moves[n].start()
     for copy in half_y:
         copy.wait_recv()
-    for copy in half_y:
-        copy.wait_send()
-    half_x_started = half_x
-    for copy in half_x_started:
+    for copy in half_x:
         copy.start()
 
     finish_recv(0, True)
@@ -273,28 +305,21 @@
     for copy in start_cols:
         copy.start()
 
-    own_moves = []
-    for s in (1, 2, 3):
-        own_y[s - 1].wait_recv()
-        copy = own_c(s)
-        copy.start()
-        own_moves.append(copy)
-    for copy in half_x:
-        copy.wait_recv()
-    for copy in half_x:
-        copy.wait_send()
-    half_c.start()
-
-    for s in (1, 2, 3):
-        y = lax.rem(iy + 4 - s, 4)
-        own_moves[s - 1].wait_recv()
-        put_operator(y, own.at[y], None)
-
+    for copy in passed:
+        copy.wait_recv()
+    own_moves.append(own_c(2))
+    own_moves[2].start()
+    for n in range(3):
+        own_moves[n].wait_recv()
+        put_operator(lax.rem(iy + (3, 1, 2)[n], 4), own.at[lax.rem(iy + (3, 1, 2)[n], 4)])
     for k in range(OPS):
         source = pl.ds(pl.multiple_of(k * SITES + half * 256, 256), 256)
         target = pl.ds(pl.multiple_of(k * SITES + (1 - half) * 256, 256), 256)
         whi[target, wide(half)] = whi[source, wide(1 - half)].T
         wlo[target, wide(half)] = wlo[source, wide(1 - half)].T
+    for copy in half_x:
+        copy.wait_recv()
+    half_c.start()
     half_c.wait_recv()
     for k in range(OPS):
         for y in range(4):
@@ -305,8 +330,6 @@
 
     for copy in start_moves:
         copy.wait_recv()
-    kept = par[OWN, 11]
-    damp = par[OWN, 10]
     first_r[...] = kept * (right(dens, 0) - damp * dens[...])
     sent_r[1] = first_r[...].T
     start_columns(1)
@@ -343,55 +366,29 @@
     second = right(first_r, 4) - damp * first_r[...]
     finish_recv(3, False)
     second = kept * (second + cols_buf[3].T)
-    out[...] = dens[...] + TIME_STEP * first_r[...] + (0.5 * TIME_STEP * TIME_STEP) * second
-
-    half_z.wait_send()
+    result = dens[...] + TIME_STEP * first_r[...] + (0.5 * TIME_STEP * TIME_STEP) * second
+    for part in range(2):
+        out[:, part, :] = result[part * ROWS:(part + 1) * ROWS]
+
+    for copy in [half_z, half_c] + half_y + half_x + passed:
+        copy.wait_send()
     for slot in range(4):
         finish_send(slot)
-    half_c.wait_send()
     for copy in keep_moves + own_y + own_moves + start_moves + start_cols + next_cols + next_moves:
         copy.wait_send()
 
 
-def parameters(rates, coupling, keep_mask):
-    occ_a = lax.axis_index("occa").astype(F32)
-    own_b = lax.axis_index("occb")
-    index_b = jnp.concatenate([jnp.arange(COUNT_B), own_b[None]])
-    occ_b = index_b.astype(F32)
-    ones = jnp.ones_like(occ_b)
-    zeros = jnp.zeros_like(occ_b)
-    up_a = jnp.where(occ_a < COUNT_A - 1, jnp.sqrt(occ_a + 1.0), 0.0) * ones
-    up_b = jnp.where(occ_b < COUNT_B - 1, jnp.sqrt(occ_b + 1.0), 0.0)
-    down_a = jnp.sqrt(occ_a) * ones
-    down_b = jnp.sqrt(occ_b)
-    damping = occ_a * rates[0] + occ_b * rates[1]
-    kept = keep_mask[0, 0].astype(F32) * ones
-    return jnp.stack(
-        [
-            zeros, -ones,
-            zeros, -up_a,
-            down_a * coupling[0, 1], -down_a * coupling[0, 0],
-            zeros, -up_b,
-            down_b * coupling[1, 1], -down_b * coupling[1, 0],
-            damping, kept,
-        ],
-        axis=1,
-    )
-
-
 def shards(density, operators, rates, coupling, keep_mask):
-    kept = keep_mask[0, 0].astype(F32)
-    start = (density[:, 0, 0] * kept).transpose(1, 0, 2).reshape(2 * ROWS, SITES)
-    keep = jnp.full((8, 128), kept, F32)
-    par = parameters(rates, coupling, keep_mask)
     vmem = pl.BlockSpec(memory_space=pltpu.VMEM)
+    smem = pl.BlockSpec(memory_space=pltpu.SMEM)
     dma = pltpu.SemaphoreType.DMA
     result = pl.pallas_call(
         kernel,
-        out_shape=jax.ShapeDtypeStruct((2 * ROWS, SITES), F32),
-        in_specs=[pl.BlockSpec(memory_space=pltpu.SMEM), vmem, vmem, vmem],
+        out_shape=jax.ShapeDtypeStruct((ROWS, 2, SITES), F32),
+        in_specs=[smem, smem, smem, vmem, vmem],
         out_specs=vmem,
         scratch_shapes=[
+            pltpu.VMEM((2 * ROWS, SITES), F32),
             pltpu.VMEM((4, OPS, ROWS, SITES), F32),
             pltpu.VMEM((4, OPS, ROWS, SITES // 2), F32),
             pltpu.VMEM((OPS * SITES, SITES), BF16),
@@ -412,14 +409,14 @@
             dma((4, 4)),
             dma((4,)),
             dma((4,)),
-            dma((14,)),
-            dma((14,)),
+            dma((15,)),
+            dma((15,)),
         ],
         compiler_params=pltpu.CompilerParams(
             collective_id=0, has_side_effects=True, vmem_limit_bytes=48 << 20
         ),
-    )(par, start, operators, keep)
-    return result.reshape(2, ROWS, SITES).transpose(1, 0, 2).reshape(density.shape)
+    )(rates, coupling, keep_mask, density.reshape(ROWS, 2, SITES), operators)
+    return result.reshape(density.shape)
 
 
 def solution(mesh):

time: 92.5 us -> 78.7 us (0.85)
  Pallas kernels: 82.7 us -> 74.5 us
  other arithmetic: 2.96 us -> 0 us
  between operations: 2.78 us -> 0.68 us
    pallas_call x1, Pallas kernels: 82.7 us -> 74.5 us  [shards(): pl.pallas_call(kernel, out_shape=jax.ShapeDtypeStruct((ROWS, 2, SITES), F...]
    unnamed x2 -> x9, local copies, waits for them, and re-layouts: 0.01 us -> 3.41 us
    slice x2 -> x0, local copies, waits for them, and re-layouts: 2.74 us -> none  [the longest x1 1.42 us: parameters(): coupling[1, 0]]
    add x1 -> x0, other arithmetic: 1.83 us -> none  [parameters(): damping = occ_a * rates[0] + occ_b * rates[1]]
    transpose x1 -> x0, other arithmetic: 1.05 us -> none  [shards(): (density[:, 0, 0] * kept).transpose(1, 0, 2).reshape(2 * ROWS, SITES)]
where the time goes in v2:
time: 78.7 us; the launch traced here: 78.6 us
  Pallas kernels  74.5 us (95%)
  local copies, waits for them, and re-layouts  3.41 us (4%)
    pallas_call x1, Pallas kernels, shards(): pl.pallas_call(kernel, out_shape=jax.ShapeDtypeStruct((ROWS, 2, SITES), F...  74.5 us
    unnamed x9, local copies, waits for them, and re-layouts  3.41 us

profile of v2, /device:TPU:1, one launch (start us, length us, event | category | flops | bytes accessed | tf_op | source)
XLA Modules:
  0.0 78.6 jit_solution(5109866493737287582)
XLA Ops:
  0.7 0.0 copy-start.2
  0.7 0.0 copy-start.3
  0.7 0.7 copy-done.2
  1.3 0.0 copy-done.3
  1.3 0.0 copy-start
  1.3 1.1 %copy-done = f32[5,64,512]{2,1,0:T(8,128)S(1)} copy-done((f32[5,64,512]{2,1,0:T(8,128)S(1)}, f32[5,64,512]{2,1,0:T(8,128)}, u32[]{:S(2)}) %copy-start) | copy-done | bytes 655384
  2.4 0.0 copy-start.1
  2.4 0.9 %copy-done.1 = f32[64,1,1,2,512]{4,3,2,1,0:T(2,128)S(1)} copy-done((f32[64,1,1,2,512]{4,3,2,1,0:T(2,128)S(1)}, f32[64,1,1,2,512]{4,3,2,1,0:T(2,128)}, u32[]{:S(2)}) %copy-start.1) | copy-done | bytes 262168
  3.4 74.5 %shard_map.55 = f32[64,2,512]{2,1,0:T(2,128)S(1)} custom-call(f32[2]{0:T(128)S(1)} %copy-done.3, f32[2,2]{1,0:T(2,128)S(1)} %copy-done.2, s32[1,1]{1,0:T(1,128)S(6)} %copy.8.mask, f32[64,2,512]{2,1,0:T(2,128)S(1)} %bitcast.5, f32[5,64,512]{2,1,0:T(8,128)S(1)} %copy-done), custom_call_target="tpu_custom_call" | custom-call | tf_op jit(solution)/shard_map/pallas_call | solution.py:385
  77.9 0.7 copy.9
Async XLA Ops:
  0.7 0.7 copy-start.2
  0.7 0.7 copy-start.3
  1.3 1.1 %copy-start = (f32[5,64,512]{2,1,0:T(8,128)S(1)}, f32[5,64,512]{2,1,0:T(8,128)}, u32[]{:S(2)}) copy-start(f32[5,64,512]{2,1,0:T(8,128)} %ops.1) | copy-start | bytes 1966084
  2.4 0.9 %copy-start.1 = (f32[64,1,1,2,512]{4,3,2,1,0:T(2,128)S(1)}, f32[64,1,1,2,512]{4,3,2,1,0:T(2,128)}, u32[]{:S(2)}) copy-start(f32[64,1,1,2,512]{4,3,2,1,0:T(2,128)} %param.5) | copy-start | bytes 786436

commit v3 on v2

--- a/solution.py
+++ b/solution.py
@@ -33,11 +33,11 @@
 
 
 def kernel(
-    rates, coupling, mask, density, ops, out,
-    dens, own, oth, whi, wlo, ghl,
+    rates, coupling, mask, density_in, ops_in, out,
+    density, ops, dens, own, oth, whi, wlo, ghl,
     sent_r, cols_buf, held_c, pack, first_r, first_c,
     near_r, near_c, keeps,
-    a_send, a_recv, n_send, n_recv, k_send, k_recv, o_send, o_recv,
+    a_send, a_recv, n_send, n_recv, k_send, k_recv, o_send, o_recv, l_sem,
 ):
     ia = lax.axis_index("occa")
     ib = lax.axis_index("occb")
@@ -61,8 +61,12 @@
         return {"rows": half * 4 + lax.rem(iy + step, 4)}
 
     def partner(j):
-        z = lax.rem(iz + j // 4, 8)
-        y = lax.rem(iy + lax.rem(j, 4), 4)
+        turn = j // 4
+        quarter = lax.rem(j, 4)
+        away = 4 + jnp.where(lax.rem(turn, 2) == 1, -((turn + 1) // 2), turn // 2)
+        aside = jnp.where(quarter < 2, 2 - quarter, jnp.where(quarter == 2, 3, 0))
+        z = lax.rem(iz + away, 8)
+        y = lax.rem(iy + aside, 4)
         b = lax.rem(z, 4)
         r = (z // 4) * 4 + y
         return {"occb": b, "rows": r}, z * 4 + y, b * 8 + r
@@ -73,10 +77,15 @@
         pl.semaphore_signal(barrier, inc=1, device_id=partner(j)[0], device_id_type=MESH)
         return carry
 
-    lax.fori_loop(1, PLANE, greet, 0)
+    lax.fori_loop(0, PLANE - 1, greet, 0)
     for step in (1, -1, 2, -2, 4):
         pl.semaphore_signal(barrier, inc=1, device_id=a_dev(step), device_id_type=MESH)
 
+    load_density = pltpu.make_async_copy(density_in, density, l_sem.at[0])
+    load_ops = pltpu.make_async_copy(ops_in, ops, l_sem.at[1])
+    load_density.start()
+    load_ops.start()
+    load_density.wait()
     kept = mask[0, 0].astype(F32)
     for part in range(2):
         dens[part * ROWS:(part + 1) * ROWS, :] = kept * density[:, part, :]
@@ -121,14 +130,14 @@
         def body(j, carry):
             to_columns(slot, j).start()
             return carry
-        lax.fori_loop(1, PLANE, body, 0)
+        lax.fori_loop(0, PLANE - 1, body, 0)
         cols_buf[slot, block(me_row), :] = sent_r[slot, block(me_col), :]
 
     def start_rows(slot):
         def body(j, carry):
             to_rows(slot, j).start()
             return carry
-        lax.fori_loop(1, PLANE, body, 0)
+        lax.fori_loop(0, PLANE - 1, body, 0)
         cols_buf[slot, block(me_col), :] = pack[slot - 2, block(me_row), :]
 
     def finish_recv(slot, by_row):
@@ -138,13 +147,13 @@
             piece = cols_buf.at[slot, block(index)]
             remote(piece, piece, a_send.at[slot, j], a_recv.at[slot, index], dev).wait_recv()
             return carry
-        lax.fori_loop(1, PLANE, body, 0)
+        lax.fori_loop(0, PLANE - 1, body, 0)
 
     def finish_send(slot):
         def body(j, carry):
             (to_columns if slot < 2 else to_rows)(slot, j).wait_send()
             return carry
-        lax.fori_loop(1, PLANE, body, 0)
+        lax.fori_loop(0, PLANE - 1, body, 0)
 
     lanes = lax.broadcasted_iota(jnp.int32, (COLS, 128), 1) < 64
 
@@ -247,10 +256,18 @@
                      o_send.at[s], o_recv.at[s], y_dev(s)) for s in (1, 2, 3)]
     half_x = [remote(oth.at[:, :, eight(share), :], oth.at[:, :, eight(share), :],
                      o_send.at[3 + s], o_recv.at[3 + s], a_dev(2 * s)) for s in (1, 2, 3)]
-    half_c = remote(oth.at[:, :, thirty_two(core), :], oth.at[:, :, thirty_two(core), :],
-                    o_send.at[7], o_recv.at[7], sibling)
-    own_y = [remote(ops.at[:, thirty_two(core), :], own.at[iy, :, thirty_two(core), :],
-                    o_send.at[8 + n], o_recv.at[8 + n], y_dev((1, 3)[n])) for n in range(2)]
+    def half_c(s):
+        rows = eight(core * 4 + lax.rem(ix + 4 - s, 4))
+        return remote(oth.at[:, :, rows, :], oth.at[:, :, rows, :],
+                      o_send.at[7 + s], o_recv.at[7 + s], sibling)
+
+    def own_y(part, n):
+        cols = slice(256 * part, 256 * part + 256)
+        return remote(ops.at[:, thirty_two(core), cols], own.at[iy, :, thirty_two(core), cols],
+                      o_send.at[11 + 2 * part + n], o_recv.at[11 + 2 * part + n], y_dev((1, 3)[n]))
+
+    own_one = [own_y(0, n) for n in range(2)]
+    own_two = [own_y(1, n) for n in range(2)]
 
     def held(n, rows):
         return own.at[lax.rem(iy + (3, 1, 2)[n], 4), :, rows, :]
@@ -259,19 +276,20 @@
         return pl.ds(pl.multiple_of(index * 16, 16), 16)
 
     passed = [remote(held(n, sixteen(2 * core + n)), held(n, sixteen(2 * core + n)),
-                     o_send.at[10 + n], o_recv.at[10 + n], y_dev((1, 3)[n])) for n in range(2)]
+                     o_send.at[15 + n], o_recv.at[15 + n], y_dev((1, 3)[n])) for n in range(2)]
 
     def own_c(n):
         return remote(held(n, thirty_two(core)), held(n, thirty_two(core)),
-                      o_send.at[12 + n], o_recv.at[12 + n], sibling)
+                      o_send.at[17 + n], o_recv.at[17 + n], sibling)
 
     keep_moves = [remote(keeps.at[ib], keeps.at[ib], k_send.at[s], k_recv.at[s],
                          {"occb": lax.rem(ib + s, COUNT_B)}) for s in (1, 2, 3)]
 
+    load_ops.wait()
     pl.semaphore_wait(barrier, PLANE - 1 + 5)
     half_z.start()
     start_columns(0)
-    for copy in own_y:
+    for copy in own_one:
         copy.start()
     start_moves = row_moves(0, dens)
     for copy in keep_moves + start_moves:
@@ -285,18 +303,13 @@
             wlo[at, :] = low
 
     half_z.wait_recv()
+    for copy in half_y + own_two:
+        copy.start()
+    put_operator(iy, ops)
     for copy in half_y:
-        copy.start()
-    put_operator(iy, ops)
-    own_moves = []
-    for n in range(2):
-        own_y[n].wait_recv()
-        passed[n].start()
-        own_moves.append(own_c(n))
-        own_moves[n].start()
-    for copy in half_y:
-        copy.wait_recv()
-    for copy in half_x:
+        copy.wait_recv()
+    half_moves = [half_c(0)]
+    for copy in half_x + half_moves:
         copy.start()
 
     finish_recv(0, True)
@@ -305,22 +318,33 @@
     for copy in start_cols:
         copy.start()
 
+    own_moves = []
+    for n in range(2):
+        own_one[n].wait_recv()
+        own_two[n].wait_recv()
+        passed[n].start()
+        own_moves.append(own_c(n))
+        own_moves[n].start()
+    for n in range(2):
+        own_moves[n].wait_recv()
+        put_operator(lax.rem(iy + (3, 1)[n], 4), own.at[lax.rem(iy + (3, 1)[n], 4)])
     for copy in passed:
         copy.wait_recv()
     own_moves.append(own_c(2))
     own_moves[2].start()
-    for n in range(3):
-        own_moves[n].wait_recv()
-        put_operator(lax.rem(iy + (3, 1, 2)[n], 4), own.at[lax.rem(iy + (3, 1, 2)[n], 4)])
+    own_moves[2].wait_recv()
+    put_operator(lax.rem(iy + 2, 4), own.at[lax.rem(iy + 2, 4)])
     for k in range(OPS):
         source = pl.ds(pl.multiple_of(k * SITES + half * 256, 256), 256)
         target = pl.ds(pl.multiple_of(k * SITES + (1 - half) * 256, 256), 256)
         whi[target, wide(half)] = whi[source, wide(1 - half)].T
         wlo[target, wide(half)] = wlo[source, wide(1 - half)].T
-    for copy in half_x:
-        copy.wait_recv()
-    half_c.start()
-    half_c.wait_recv()
+    for s in (1, 3, 2):
+        half_x[s - 1].wait_recv()
+        half_moves.append(half_c(s))
+        half_moves[-1].start()
+    for copy in half_moves:
+        copy.wait_recv()
     for k in range(OPS):
         for y in range(4):
             at = pl.ds(pl.multiple_of(k * SITES + (1 - half) * 256 + y * ROWS, ROWS), ROWS)
@@ -370,24 +394,27 @@
     for part in range(2):
         out[:, part, :] = result[part * ROWS:(part + 1) * ROWS]
 
-    for copy in [half_z, half_c] + half_y + half_x + passed:
+    for copy in [half_z] + half_y + half_x + half_moves + passed + own_one + own_two:
         copy.wait_send()
     for slot in range(4):
         finish_send(slot)
-    for copy in keep_moves + own_y + own_moves + start_moves + start_cols + next_cols + next_moves:
+    for copy in keep_moves + own_moves + start_moves + start_cols + next_cols + next_moves:
         copy.wait_send()
 
 
 def shards(density, operators, rates, coupling, keep_mask):
     vmem = pl.BlockSpec(memory_space=pltpu.VMEM)
     smem = pl.BlockSpec(memory_space=pltpu.SMEM)
+    hbm = pl.BlockSpec(memory_space=pl.ANY)
     dma = pltpu.SemaphoreType.DMA
     result = pl.pallas_call(
         kernel,
         out_shape=jax.ShapeDtypeStruct((ROWS, 2, SITES), F32),
-        in_specs=[smem, smem, smem, vmem, vmem],
+        in_specs=[smem, smem, smem, hbm, hbm],
         out_specs=vmem,
         scratch_shapes=[
+            pltpu.VMEM((ROWS, 2, SITES), F32),
+            pltpu.VMEM((OPS, ROWS, SITES), F32),
             pltpu.VMEM((2 * ROWS, SITES), F32),
             pltpu.VMEM((4, OPS, ROWS, SITES), F32),
             pltpu.VMEM((4, OPS, ROWS, SITES // 2), F32),
@@ -409,11 +436,12 @@
             dma((4, 4)),
             dma((4,)),
             dma((4,)),
-            dma((15,)),
-            dma((15,)),
+            dma((20,)),
+            dma((20,)),
+            dma((2,)),
         ],
         compiler_params=pltpu.CompilerParams(
-            collective_id=0, has_side_effects=True, vmem_limit_bytes=48 << 20
+            collective_id=0, has_side_effects=True, vmem_limit_bytes=60 << 20
         ),
     )(rates, coupling, keep_mask, density.reshape(ROWS, 2, SITES), operators)
     return result.reshape(density.shape)

time: 78.7 us -> 73 us (0.928)
  Pallas kernels: 74.5 us -> 70.5 us
  local copies, waits for them, and re-layouts: 3.41 us -> 1.67 us
    pallas_call x1, Pallas kernels: 74.5 us -> 70.5 us  [shards(): pl.pallas_call(kernel, out_shape=jax.ShapeDtypeStruct((ROWS, 2, SITES), F...]
    unnamed x9 -> x1, local copies, waits for them, and re-layouts: 3.41 us -> 1.67 us
where the time goes in v3:
time: 73 us; the launch traced here: 72.8 us
  Pallas kernels  70.5 us (97%)
  local copies, waits for them, and re-layouts  1.67 us (2%)
    pallas_call x1, Pallas kernels, shards(): pl.pallas_call(kernel, out_shape=jax.ShapeDtypeStruct((ROWS, 2, SITES), F...  70.5 us
    unnamed x1, local copies, waits for them, and re-layouts  1.67 us

profile of v3, /device:TPU:1, one launch (start us, length us, event | category | flops | bytes accessed | tf_op | source)
XLA Modules:
  0.0 72.8 jit_solution(9277927577359706668)
XLA Ops:
  0.7 70.5 %shard_map.55 = f32[64,2,512]{2,1,0:T(2,128)} custom-call(f32[2]{0:T(128)} %rates.1, f32[2,2]{1,0:T(2,128)} %coupling.1, s32[1,1]{1,0:T(1,128)S(6)} %copy.8.mask, f32[64,2,512]{2,1,0:T(2,128)} %bitcast.5, f32[5,64,512]{2,1,0:T(8,128)} %ops_in.1), custom_call_target="tpu_custom_call" | custom-call | tf_op jit(solution)/shard_map/pallas_call | solution.py:410
  71.1 1.7 %copy.9 = f32[64,1,1,2,512]{4,3,2,1,0:T(2,128)} copy(f32[64,1,1,2,512]{4,3,2,1,0:T(2,128)} %bitcast.4) | data formatting | bytes 524288

commit v4 on v3

v4 whole, which is shorter than its diff:
```python
import math
import jax
import jax.numpy as jnp
from jax import lax
from jax.experimental import pallas as pl
from jax.experimental.pallas import tpu as pltpu
from jax.sharding import PartitionSpec as P

TIME_STEP = 0.05
MESH = pl.DeviceIdType.MESH
F32 = jnp.float32
BF16 = jnp.bfloat16
SITES = 512
OPS = 5
ROWS = 64
COLS = 16
PLANE = 32
COUNT_A = 8
COUNT_B = 4


def split(value):
    high = value.astype(BF16)
    low = (value - high.astype(F32)).astype(BF16)
    return high, low


def root(count):
    value = jnp.float32(0.0)
    for n in range(1, COUNT_A):
        value = jnp.where(count == n, math.sqrt(n), value)
    return value


def kernel(
    rates_in, coupling_in, mask, density_in, ops_in, out,
    rates, coupling, density, ops, dens, own, oth, whi, wlo, ghl,
    sent_r, cols_buf, held_c, pack, first_r, first_c,
    near_r, near_c, keeps,
    a_send, a_recv, n_send, n_recv, k_send, k_recv, o_send, o_recv, l_sem,
):
    ia = lax.axis_index("occa")
    ib = lax.axis_index("occb")
    ir = lax.axis_index("rows")
    half = ir // 4
    iy = lax.rem(ir, 4)
    ix = ia // 2
    core = lax.rem(ia, 2)
    iz = half * 4 + ib
    me_col = iz * 4 + iy
    me_row = ib * 8 + ir

    far, near = 1 - half, half

    def a_dev(step):
        return {"occa": lax.rem(ia + step + COUNT_A, COUNT_A)}

    def z_dev(step):
        z = lax.rem(iz + step + 8, 8)
        return {"occb": lax.rem(z, 4), "rows": (z // 4) * 4 + iy}

    def y_dev(step):
        return {"rows": half * 4 + lax.rem(iy + step, 4)}

    def partner(j):
        turn = j // 4
        quarter = lax.rem(j, 4)
        away = 4 + jnp.where(lax.rem(turn, 2) == 1, -((turn + 1) // 2), turn // 2)
        aside = jnp.where(quarter < 2, 2 - quarter, jnp.where(quarter == 2, 3, 0))
        z = lax.rem(iz + away, 8)
        y = lax.rem(iy + aside, 4)
        b = lax.rem(z, 4)
        r = (z // 4) * 4 + y
        return {"occb": b, "rows": r}, z * 4 + y, b * 8 + r

    def half_partner(j):
        turn = lax.rem(j // 4, 4)
        quarter = lax.rem(j, 4)
        aside = jnp.where(quarter < 2, 2 - quarter, jnp.where(quarter == 2, 3, 0))
        b = lax.rem(ib + jnp.where(j < 16, turn, 3 - turn), COUNT_B)
        y = lax.rem(iy + aside, 4)
        group = jnp.where(j < 16, far, near)
        r = group * 4 + y
        return {"occb": b, "rows": r}, (group * 4 + b) * 4 + y, b * 8 + r

    barrier = pltpu.get_barrier_semaphore()

    def greet(j, carry):
        pl.semaphore_signal(barrier, inc=1, device_id=partner(j)[0], device_id_type=MESH)
        return carry

    lax.fori_loop(0, PLANE - 1, greet, 0)
    for step in (1, -1, 2, -2, 4):
        pl.semaphore_signal(barrier, inc=1, device_id=a_dev(step), device_id_type=MESH)

    load_density = pltpu.make_async_copy(density_in, density, l_sem.at[0])
    load_ops = pltpu.make_async_copy(ops_in, ops, l_sem.at[1])
    load_rates = pltpu.make_async_copy(rates_in, rates, l_sem.at[2])
    load_coupling = pltpu.make_async_copy(coupling_in, coupling, l_sem.at[3])
    load_density.start()
    load_rates.start()
    load_coupling.start()
    load_ops.start()
    load_density.wait()
    kept = mask[0, 0].astype(F32)
    for part in range(2):
        dens[part * ROWS:(part + 1) * ROWS, :] = kept * density[:, part, :]
    sent_r[0] = dens[...].T
    keeps[ib] = jnp.full((8, 128), kept, F32)
    load_rates.wait()
    load_coupling.wait()
    down_a = root(ia)
    up_a = jnp.where(ia < COUNT_A - 1, root(ia + 1), 0.0)
    damp = ia.astype(F32) * rates[0] + ib.astype(F32) * rates[1]

    def factors(b):
        down_b = root(b)
        up_b = jnp.where(b < COUNT_B - 1, root(b + 1), 0.0)
        return [
            (0.0, -1.0),
            (0.0, -up_a),
            (down_a * coupling[0, 1], -down_a * coupling[0, 0]),
            (0.0, -up_b),
            (down_b * coupling[1, 1], -down_b * coupling[1, 0]),
        ]

    sibling = {"occa": ix * 2 + 1 - core}

    def remote(src, dst, send, recv, dev):
        return pltpu.make_async_remote_copy(
            src_ref=src, dst_ref=dst, send_sem=send, recv_sem=recv, device_id=dev, device_id_type=MESH
        )

    def block(index):
        return pl.ds(pl.multiple_of(index * COLS, COLS), COLS)

    def target(slot, j):
        return half_partner(j) if slot in (1, 2) else partner(j)

    def to_columns(slot, j):
        dev, col, row = target(slot, j)
        return remote(sent_r.at[slot, block(col)], cols_buf.at[slot, block(me_row)],
                      a_send.at[slot, j], a_recv.at[slot, me_row], dev)

    def to_rows(slot, j):
        dev, col, row = target(slot, j)
        return remote(pack.at[slot - 2, block(row)], cols_buf.at[slot, block(me_col)],
                      a_send.at[slot, j], a_recv.at[slot, me_col], dev)

    def start_columns(slot, first=0, last=PLANE - 1):
        def body(j, carry):
            to_columns(slot, j).start()
            return carry
        lax.fori_loop(first, last, body, 0)
        if last == PLANE - 1:
            cols_buf[slot, block(me_row), :] = sent_r[slot, block(me_col), :]

    def start_rows(slot, first=0, last=PLANE - 1):
        def body(j, carry):
            to_rows(slot, j).start()
            return carry
        lax.fori_loop(first, last, body, 0)
        if last == PLANE - 1:
            cols_buf[slot, block(me_col), :] = pack[slot - 2, block(me_row), :]

    def finish_recv(slot, by_row):
        def body(j, carry):
            dev, col, row = target(slot, j)
            index = row if by_row else col
            piece = cols_buf.at[slot, block(index)]
            remote(piece, piece, a_send.at[slot, j], a_recv.at[slot, index], dev).wait_recv()
            return carry
        lax.fori_loop(0, PLANE - 1, body, 0)

    def finish_send(slot):
        def body(j, carry):
            (to_columns if slot < 2 else to_rows)(slot, j).wait_send()
            return carry
        lax.fori_loop(0, PLANE - 1, body, 0)

    lanes = lax.broadcasted_iota(jnp.int32, (COLS, 128), 1) < 64

    def unpack(slot):
        parts = []
        for b in range(COUNT_B):
            real, imag = [], []
            for t in range(4):
                q = (b * 8 + 2 * t) * COLS
                even = cols_buf[slot, q:q + COLS, :]
                odd = cols_buf[slot, q + COLS:q + 2 * COLS, :]
                real.append(jnp.where(lanes, even, pltpu.roll(odd, 64, 1)))
                imag.append(jnp.where(lanes, pltpu.roll(even, 64, 1), odd))
            parts.append(jnp.concatenate(real, axis=1))
            parts.append(jnp.concatenate(imag, axis=1))
        return jnp.concatenate(parts, axis=0)

    def repack(slot, value, group=0):
        for b in range(COUNT_B):
            for t in range(value.shape[1] // 128):
                real = value[32 * b:32 * b + COLS, 128 * t:128 * t + 128]
                imag = value[32 * b + COLS:32 * b + 32, 128 * t:128 * t + 128]
                q = b * 8 + group * 4 + 2 * t
                pack[slot - 2, block(q), :] = jnp.where(lanes, real, pltpu.roll(imag, 64, 1))
                pack[slot - 2, block(q + 1), :] = jnp.where(lanes, pltpu.roll(real, 64, 1), imag)

    def put(side, k, row, value):
        high, low = split(value)
        count = value.shape[0]
        ghl[side, row:row + count, k * SITES:(k + 1) * SITES] = high
        ghl[side, 128 + row:128 + row + count, k * SITES:(k + 1) * SITES] = low

    def multiply(side, cols=slice(None)):
        both = jnp.dot(ghl[side], whi[:, cols], preferred_element_type=F32)
        rest = jnp.dot(ghl[side, 0:128, :], wlo[:, cols], preferred_element_type=F32)
        return both[0:128] + both[128:256] + rest

    def right(center, base):
        fields = [center, near_r.at[base], near_r.at[base + 1], near_r.at[base + 2], near_r.at[base + 3]]
        own_factors = factors(ib)
        for k, field in enumerate(fields):
            re, im = field[0:ROWS, :], field[ROWS:128, :]
            f_re, f_im = own_factors[k]
            put(0, k, 0, f_re * re + f_im * im)
            put(0, k, ROWS, f_re * im - f_im * re)

    def left(center, base):
        for b in range(COUNT_B):
            b_factors = factors(b)
            for k in range(OPS):
                source, at = center, b
                if k == 1:
                    source = near_c.at[base]
                elif k == 2:
                    source = near_c.at[base + 1]
                elif k == 3:
                    at = min(b + 1, COUNT_B - 1)
                elif k == 4:
                    at = max(b - 1, 0)
                re = source[32 * at:32 * at + COLS, :]
                im = source[32 * at + COLS:32 * at + 32, :]
                f_re, f_im = b_factors[k]
                put(1, k, 32 * b, f_re * re - f_im * im)
                put(1, k, 32 * b + COLS, f_re * im + f_im * re)

    def near_copy(kind, index, src, dst, dev):
        return remote(src, dst, n_send.at[kind, index], n_recv.at[kind, index], dev)

    def row_moves(kind, src):
        base = 4 * kind
        return [
            near_copy(kind, 0, src, near_r.at[base], a_dev(-1)),
            near_copy(kind, 1, src, near_r.at[base + 1], a_dev(1)),
            near_copy(kind, 2, src, near_r.at[base + 2], z_dev(-1)),
            near_copy(kind, 3, src, near_r.at[base + 3], z_dev(1)),
        ]

    def col_moves(kind, src):
        base = 2 * kind
        return [
            near_copy(2 + kind, 0, src, near_c.at[base], a_dev(-1)),
            near_copy(2 + kind, 1, src, near_c.at[base + 1], a_dev(1)),
        ]

    def eight(index):
        return pl.ds(pl.multiple_of(index * 8, 8), 8)

    def thirty_two(index):
        return pl.ds(pl.multiple_of(index * 32, 32), 32)

    def wide(index):
        return pl.ds(pl.multiple_of(index * 256, 256), 256)

    def sixteen(index):
        return pl.ds(pl.multiple_of(index * 16, 16), 16)

    parity = lax.rem(ix, 2)
    shares = [eight(core * 4 + parity * 2 + n) for n in range(2)]
    others = [eight(core * 4 + (1 - parity) * 2 + n) for n in range(2)]
    half_z = [remote(ops.at[:, shares[n], wide(half)], oth.at[iy, :, shares[n], :],
                     o_send.at[n], o_recv.at[n], z_dev(4)) for n in range(2)]
    half_y = [[remote(oth.at[iy, :, shares[n], :], oth.at[iy, :, shares[n], :],
                      o_send.at[1 + 3 * n + s], o_recv.at[1 + 3 * n + s], y_dev(s)) for s in (2, 1, 3)]
              for n in range(2)]
    half_x = [remote(oth.at[:, :, shares[n], :], oth.at[:, :, shares[n], :],
                     o_send.at[8 + n], o_recv.at[8 + n], a_dev((-2, 2)[n])) for n in range(2)]
    half_c = [remote(oth.at[:, :, rows, :], oth.at[:, :, rows, :],
                     o_send.at[10 + n], o_recv.at[10 + n], sibling) for n, rows in enumerate(shares + others)]

    groups = (far, near)

    def own_y(part, n):
        return remote(ops.at[:, thirty_two(core), wide(groups[part])],
                      own.at[iy, :, thirty_two(core), wide(groups[part])],
                      o_send.at[14 + 2 * part + n], o_recv.at[14 + 2 * part + n], y_dev((1, 3)[n]))

    def held(part, n, rows):
        return own.at[lax.rem(iy + (3, 1, 2)[n], 4), :, rows, wide(groups[part])]

    def passed_y(part, n):
        piece = held(part, n, sixteen(2 * core + n))
        return remote(piece, piece, o_send.at[18 + 2 * part + n], o_recv.at[18 + 2 * part + n], y_dev((1, 3)[n]))

    def own_c(part, n):
        piece = held(part, n, thirty_two(core))
        return remote(piece, piece, o_send.at[22 + 3 * part + n], o_recv.at[22 + 3 * part + n], sibling)

    own_moves = [[own_y(part, n) for n in range(2)] for part in range(2)]
    passed = [[passed_y(part, n) for n in range(2)] for part in range(2)]
    own_pairs = [[own_c(part, n) for n in range(3)] for part in range(2)]

    keep_moves = [remote(keeps.at[ib], keeps.at[ib], k_send.at[s], k_recv.at[s],
                         {"occb": lax.rem(ib + s, COUNT_B)}) for s in (1, 2, 3)]

    load_ops.wait()
    pl.semaphore_wait(barrier, PLANE - 1 + 5)
    for copy in half_z:
        copy.start()
    start_columns(0)
    for copy in own_moves[0]:
        copy.start()
    start_moves = row_moves(0, dens)
    for copy in keep_moves + start_moves:
        copy.start()

    def put_operator(part, y, rows):
        cols = wide(groups[part])
        for k in range(OPS):
            at = pl.ds(pl.multiple_of(k * SITES + half * 256 + y * ROWS, ROWS), ROWS)
            high, low = split(rows[k, :, cols])
            whi[at, cols] = high
            wlo[at, cols] = low

    def pass_on(part):
        for n in range(2):
            own_moves[part][n].wait_recv()
            passed[part][n].start()
            own_pairs[part][n].start()

    def put_own(part):
        for n in range(2):
            own_pairs[part][n].wait_recv()
            y = lax.rem(iy + (3, 1)[n], 4)
            put_operator(part, y, own.at[y])
        for copy in passed[part]:
            copy.wait_recv()
        own_pairs[part][2].start()
        own_pairs[part][2].wait_recv()
        y = lax.rem(iy + 2, 4)
        put_operator(part, y, own.at[y])

    half_z[0].wait_recv()
    for copy in half_y[0]:
        copy.start()
    put_operator(0, iy, ops)
    half_z[1].wait_recv()
    for copy in half_y[1]:
        copy.start()
    pass_on(0)
    for copy in own_moves[1]:
        copy.start()

    finish_recv(0, True)
    held_c[...] = unpack(0)
    start_cols = col_moves(0, held_c)
    for copy in start_cols:
        copy.start()
    for n in range(2):
        for copy in half_y[n]:
            copy.wait_recv()
        half_x[n].start()
        half_c[n].start()

    put_own(0)
    put_operator(1, iy, ops)
    pass_on(1)
    for copy in start_moves:
        copy.wait_recv()
    right(dens, 0)
    for n in range(2):
        half_x[n].wait_recv()
        half_c[2 + n].start()
    for copy in half_c:
        copy.wait_recv()
    for k in range(OPS):
        for y in range(4):
            at = pl.ds(pl.multiple_of(k * SITES + far * 256 + y * ROWS, ROWS), ROWS)
            high, low = split(oth[y, k])
            whi[at, wide(far)] = high
            wlo[at, wide(far)] = low

    def first_right(part):
        cols = wide(groups[part])
        value = kept * (multiply(0, cols) - damp * dens[:, cols])
        first_r[:, cols] = value
        sent_r[1, cols, :] = value.T
        start_columns(1, 16 * part, 16 + 15 * part)

    def first_left(part):
        cols = wide(groups[part])
        value = kept_c * multiply(1, cols)
        first_c[:, cols] = value
        repack(2, value, groups[part])
        start_rows(2, 16 * part, 16 + 15 * part)

    first_right(0)
    for copy in start_cols:
        copy.wait_recv()
    for copy in keep_moves:
        copy.wait_recv()
    kept_c = jnp.concatenate(
        [jnp.broadcast_to(keeps[b, 0:1, 0:1], (2 * COLS, SITES // 2)) for b in range(COUNT_B)], axis=0
    )
    left(held_c, 0)
    first_left(0)

    put_own(1)
    for k in range(OPS):
        source = pl.ds(pl.multiple_of(k * SITES + near * 256, 256), 256)
        target_rows = pl.ds(pl.multiple_of(k * SITES + far * 256, 256), 256)
        whi[target_rows, wide(near)] = whi[source, wide(far)].T
        wlo[target_rows, wide(near)] = wlo[source, wide(far)].T
    first_right(1)
    first_left(1)

    finish_recv(1, True)
    first_c[...] += unpack(1)
    next_cols = col_moves(1, first_c)
    for copy in next_cols:
        copy.start()
    finish_recv(2, False)
    first_r[...] += cols_buf[2].T
    next_moves = row_moves(1, first_r)
    for copy in next_moves:
        copy.start()

    for copy in next_cols:
        copy.wait_recv()
    left(first_c, 2)
    repack(3, multiply(1))
    start_rows(3)

    for copy in next_moves:
        copy.wait_recv()
    right(first_r, 4)
    second = multiply(0) - damp * first_r[...]
    finish_recv(3, False)
    second = kept * (second + cols_buf[3].T)
    result = dens[...] + TIME_STEP * first_r[...] + (0.5 * TIME_STEP * TIME_STEP) * second
    for part in range(2):
        out[:, part, :] = result[part * ROWS:(part + 1) * ROWS]

    for copy in half_z + half_y[0] + half_y[1] + half_x + half_c:
        copy.wait_send()
    for slot in range(4):
        finish_send(slot)
    for part in range(2):
        for copy in own_moves[part] + passed[part] + own_pairs[part]:
            copy.wait_send()
    for copy in keep_moves + start_moves + start_cols + next_cols + next_moves:
        copy.wait_send()


def shards(density, operators, rates, coupling, keep_mask):
    vmem = pl.BlockSpec(memory_space=pltpu.VMEM)
    smem = pl.BlockSpec(memory_space=pltpu.SMEM)
    hbm = pl.BlockSpec(memory_space=pl.ANY)
    dma = pltpu.SemaphoreType.DMA
    result = pl.pallas_call(
        kernel,
        out_shape=jax.ShapeDtypeStruct((ROWS, 2, SITES), F32),
        in_specs=[hbm, hbm, smem, hbm, hbm],
        out_specs=vmem,
        scratch_shapes=[
            pltpu.SMEM((2,), F32),
            pltpu.SMEM((2, 2), F32),
            pltpu.VMEM((ROWS, 2, SITES), F32),
            pltpu.VMEM((OPS, ROWS, SITES), F32),
            pltpu.VMEM((2 * ROWS, SITES), F32),
            pltpu.VMEM((4, OPS, ROWS, SITES), F32),
            pltpu.VMEM((4, OPS, ROWS, SITES // 2), F32),
            pltpu.VMEM((OPS * SITES, SITES), BF16),
            pltpu.VMEM((OPS * SITES, SITES), BF16),
            pltpu.VMEM((2, 256, OPS * SITES), BF16),
            pltpu.VMEM((2, SITES, 128), F32),
            pltpu.VMEM((4, SITES, 128), F32),
            pltpu.VMEM((128, SITES), F32),
            pltpu.VMEM((2, SITES, 128), F32),
            pltpu.VMEM((128, SITES), F32),
            pltpu.VMEM((128, SITES), F32),
            pltpu.VMEM((8, 128, SITES), F32),
            pltpu.VMEM((4, 128, SITES), F32),
            pltpu.VMEM((COUNT_B, 8, 128), F32),
            dma((4, PLANE)),
            dma((4, PLANE)),
            dma((4, 4)),
            dma((4, 4)),
            dma((4,)),
            dma((4,)),
            dma((28,)),
            dma((28,)),
            dma((4,)),
        ],
        compiler_params=pltpu.CompilerParams(
            collective_id=0, has_side_effects=True, vmem_limit_bytes=60 << 20
        ),
    )(rates, coupling, keep_mask, density.reshape(ROWS, 2, SITES), operators)
    return result.reshape(density.shape)


def solution(mesh):
    placed = (
        P("rows", "occa", "occb", None, None),
        P(None, "rows", None),
        P(),
        P(),
        P("occa", "occb"),
    )
    return jax.shard_map(
        shards,
        mesh=mesh,
        in_specs=placed,
        out_specs=P("rows", "occa", "occb", None, None),
        check_vma=False,
    )
```

time: 73 us -> 70.9 us (0.971)
  the two profiles are of different devices: /device:TPU:1 before, /device:TPU:8 now
where the time goes in v4:
time: 70.9 us; the launch traced here: 70.8 us
  Pallas kernels  68.5 us (97%)
  local copies, waits for them, and re-layouts  1.67 us (2%)
    pallas_call x1, Pallas kernels, shards(): pl.pallas_call(kernel, out_shape=jax.ShapeDtypeStruct((ROWS, 2, SITES), F...  68.5 us
    unnamed x1, local copies, waits for them, and re-layouts  1.67 us

profile of v4, /device:TPU:8, one launch (start us, length us, event | category | flops | bytes accessed | tf_op | source)
XLA Modules:
  0.0 70.8 jit_solution(11875800213598588397)
XLA Ops:
  0.7 68.5 %shard_map.55 = f32[64,2,512]{2,1,0:T(2,128)} custom-call(f32[2]{0:T(128)} %rates_in.1, f32[2,2]{1,0:T(2,128)} %coupling_in.1, s32[1,1]{1,0:T(1,128)S(6)} %copy.8.mask, f32[64,2,512]{2,1,0:T(2,128)} %bitcast.5, f32[5,64,512]{2,1,0:T(8,128)} %ops_in.1), custom_call_target="tpu_custom_call" | custom-call | tf_op jit(solution)/shard_map/pallas_call | solution.py:468
  69.1 1.7 %copy.9 = f32[64,1,1,2,512]{4,3,2,1,0:T(2,128)} copy(f32[64,1,1,2,512]{4,3,2,1,0:T(2,128)} %bitcast.4) | data formatting | bytes 524288
